TPU v7x, 768 devices: a whole 4x8x12 slice. The times are simulated.
768 devices in a mesh: ctx: 64 (over x, y, core), inner: 12 (over z).
Axes of the slice: x: 4, y: 8, z: 12, core: 2. Of those that a mesh axis runs over, the one named last changes fastest.
Arguments:
- low_rank: bfloat16 [49152, 32], P(('ctx', 'inner')), may hold values from -6 to 6
- q_base: bfloat16 [49152, 4608], P(('ctx', 'inner')), may hold values from -6 to 6
- k_base: bfloat16 [49152, 4608], P(('ctx', 'inner')), may hold values from -6 to 6
- v_base: bfloat16 [49152, 4608], P(('ctx', 'inner')), may hold values from -6 to 6
- edit_up: bfloat16 [32, 13824], replicated, may hold values from -0.5 to 0.5
- log_decay: bfloat16 [49152, 36], P(('ctx', 'inner')), may hold values from -1 to 0
- lengths: int32 [64], P('ctx'), may hold values from 384 to 768, as said below
- norm_gain: float32 [4608], replicated, may hold values from 0.5 to 1.5
Outputs:
- attended: bfloat16 [49152, 4608], P(('ctx', 'inner'))
Inputs may be any that keep to these rules, and one draw needn't show every extreme that they name: `lengths`: every segment keeps at least half of its tokens, and some segment is full.
All inputs are finite; a program needn't handle non-finite values.
Results may differ from a plain program's by a relative error of at most 0.0072.
Values may be sent and summed in bfloat16 or wider, within the bound.
A program may use at most 64 MiB of HBM per device.

v0:
```python
import math

import jax
import jax.numpy as jnp
from jax import lax
from jax.sharding import PartitionSpec as P


def carried_in(value, axis, join, neutral):
    count, mine = (lax.axis_size(axis), lax.axis_index(axis))
    pieces = jax.tree.map(lambda part: lax.all_gather(part, axis), value)
    so_far = jax.tree.map(
        lambda part, zero: jnp.full_like(part, 0) + jnp.asarray(zero, part.dtype), value, neutral
    )

    def hop(position, so_far):
        longer = join(so_far, jax.tree.map(lambda part: part[position], pieces))
        return jax.tree.map(lambda new, old: jnp.where(position < mine, new, old), longer, so_far)

    return lax.fori_loop(0, count - 1, hop, so_far)


def combine(earlier, later):
    return (earlier[0] * later[0], later[0][:, None, None] * earlier[1] + later[1])


def rows_to_heads(rows):
    return lax.all_to_all(rows, "inner", split_axis=1, concat_axis=0, tiled=True)


def shards(low_rank, q_base, k_base, v_base, edit_up, log_decay, lengths, norm_gain):
    row_count = q_base.shape[0]
    full_width = q_base.shape[1]
    head_count = log_decay.shape[1]
    groups = lax.axis_size("inner")
    local_heads = head_count // groups
    head_dim = full_width // head_count
    segment_rows = row_count * groups
    tile_count = math.gcd(groups, max(1, segment_rows // 512))
    block_rows = segment_rows // tile_count
    positions = lax.axis_index("inner") * row_count + jnp.arange(row_count, dtype=jnp.int32)
    live_rows = (positions < lengths[0])[:, None]

    def edit_part(column):
        factor = edit_up[:, column * full_width : (column + 1) * full_width]
        return jnp.dot(low_rank, factor, preferred_element_type=jnp.float32)

    queries = (q_base.astype(jnp.float32) + edit_part(0)).astype(jnp.bfloat16)
    keys_all = jnp.where(live_rows, k_base.astype(jnp.float32) + edit_part(1), 0.0).astype(
        jnp.bfloat16
    )
    values_all = jnp.where(live_rows, v_base.astype(jnp.float32) + edit_part(2), 0.0).astype(
        jnp.bfloat16
    )
    key_cols, decay_cols = (
        lax.all_to_all(keys_all, "inner", split_axis=1, concat_axis=0, tiled=True),
        lax.all_to_all(log_decay, "inner", split_axis=1, concat_axis=0, tiled=True),
    )
    query_cols = rows_to_heads(queries)
    value_cols = rows_to_heads(values_all)
    key_heads = key_cols.reshape(segment_rows, local_heads, head_dim)
    value_heads = value_cols.reshape(segment_rows, local_heads, head_dim)
    decay_sum = jnp.cumsum(decay_cols.astype(jnp.float32), axis=0)
    ending = decay_sum[-1]
    scaled = (
        key_heads.astype(jnp.float32) * jnp.exp(ending[None, :] - decay_sum)[:, :, None]
    ).astype(jnp.bfloat16)
    seg_state = jnp.einsum("shd,she->hde", scaled, value_heads, preferred_element_type=jnp.float32)
    query_heads = query_cols.reshape(segment_rows, local_heads, head_dim)
    sum_heads = decay_sum.T
    order_ids = jnp.arange(block_rows, dtype=jnp.int32)
    causal = (order_ids[:, None] >= order_ids[None, :])[None]
    identity = (
        jnp.ones((local_heads,), jnp.float32),
        jnp.zeros((local_heads, head_dim, head_dim), jnp.float32),
    )
    total_decay, former = carried_in((jnp.exp(ending), seg_state), "ctx", combine, identity)
    scores = jnp.einsum("thd,shd->hts", query_heads, key_heads, preferred_element_type=jnp.float32)
    gap_log = sum_heads[:, 0:block_rows, None] - sum_heads[:, None, 0:block_rows]
    weights = jnp.where(causal, scores * jnp.exp(jnp.where(causal, gap_log, 0.0)), 0.0).astype(
        jnp.bfloat16
    )
    total = jnp.einsum("hts,shd->thd", weights, value_heads, preferred_element_type=jnp.float32)
    inter_term = jnp.exp(decay_sum)[:, :, None] * jnp.einsum(
        "thd,hde->the", query_heads, former.astype(jnp.bfloat16), preferred_element_type=jnp.float32
    )
    mixed_out = (
        (total + inter_term).astype(jnp.bfloat16).reshape(segment_rows, local_heads * head_dim)
    )
    token_out = lax.all_to_all(mixed_out, "inner", split_axis=0, concat_axis=1, tiled=True)
    token_out = jnp.where(live_rows, token_out, jnp.zeros_like(token_out))
    flat_out = token_out.astype(jnp.float32)
    inv_rms = lax.rsqrt(jnp.mean(flat_out * flat_out, axis=-1, keepdims=True) + 1e-06)
    return (flat_out * inv_rms * norm_gain[None, :]).astype(jnp.bfloat16)


def solution(mesh):
    return jax.shard_map(
        shards,
        mesh=mesh,
        in_specs=(
            P(("ctx", "inner"), None),
            P(("ctx", "inner"), None),
            P(("ctx", "inner"), None),
            P(("ctx", "inner"), None),
            P(),
            P(("ctx", "inner"), None),
            P("ctx"),
            P(),
        ),
        out_specs=P(("ctx", "inner"), None),
        check_vma=False,
    )
```

profile of v0, /device:TPU:8, one launch (start us, length us, event | category | flops | bytes accessed | tf_op | source)
XLA Modules:
  0.0 346.1 jit_solution(11349887384317013634)
XLA Ops:
  6.5 1.3 all_to_all.69
  7.9 15.2 %all-to-all-start.3 = ((bf16[64,12,3]{0,2,1:T(4,128)(2,1)}), bf16[64,12,3]{0,2,1:T(4,128)(2,1)S(1)}, u32[]{:S(2)}, u32[]{:S(2)}) async-start(bf16[64,12,3]{0,2,1:T(4,128)(2,1)} %all_to_all.69), calls=%async_computation.3 | async-start | bytes 24576 | tf_op jit(solution)/shard_map/all_to_all | solution.py:57
  23.7 1.5 fusion.5
  26.1 7.0 %all-to-all-done.3 = bf16[64,12,3]{0,2,1:T(4,128)(2,1)S(1)} async-done(((bf16[64,12,3]{0,2,1:T(4,128)(2,1)}), bf16[64,12,3]{0,2,1:T(4,128)(2,1)S(1)}, u32[]{:S(2)}, u32[]{:S(2)}) %all-to-all-start.3) | async-done | bytes 4640 | tf_op jit(solution)/shard_map/all_to_all | solution.py:57
  33.1 3.6 %all-to-all-start.2 = ((bf16[64,12,384]{2,0,1:T(8,128)(2,1)}), bf16[64,12,384]{2,0,1:T(8,128)(2,1)S(1)}, u32[]{:S(2)}, u32[]{:S(2)}) async-start(bf16[64,12,384]{2,0,1:T(8,128)(2,1)} %bitcast.62), calls=%async_computation.2 | async-start | bytes 1179648 | tf_op jit(solution)/shard_map/all_to_all | solution.py:56
  38.0 25.1 %all-to-all-done.2 = bf16[64,12,384]{2,0,1:T(8,128)(2,1)S(1)} async-done(((bf16[64,12,384]{2,0,1:T(8,128)(2,1)}), bf16[64,12,384]{2,0,1:T(8,128)(2,1)S(1)}, u32[]{:S(2)}, u32[]{:S(2)}) %all-to-all-start.2) | async-done | bytes 589856 | tf_op jit(solution)/shard_map/all_to_all | solution.py:56
  63.1 3.6 %all-to-all-start = ((bf16[64,12,384]{2,0,1:T(8,128)(2,1)}), bf16[64,12,384]{2,0,1:T(8,128)(2,1)S(1)}, u32[]{:S(2)}, u32[]{:S(2)}) async-start(bf16[64,12,384]{2,0,1:T(8,128)(2,1)} %bitcast.64), calls=%async_computation | async-start | bytes 1179648 | tf_op jit(solution)/shard_map/all_to_all | solution.py:28
  69.4 21.1 %all-to-all-done = bf16[64,12,384]{2,0,1:T(8,128)(2,1)S(1)} async-done(((bf16[64,12,384]{2,0,1:T(8,128)(2,1)}), bf16[64,12,384]{2,0,1:T(8,128)(2,1)S(1)}, u32[]{:S(2)}, u32[]{:S(2)}) %all-to-all-start) | async-done | bytes 589856 | tf_op jit(solution)/shard_map/all_to_all | solution.py:28
  92.7 1.1 fusion.14
  95.0 4.2 %all-to-all-start.1 = ((bf16[64,12,384]{2,0,1:T(8,128)(2,1)}), bf16[64,12,384]{2,0,1:T(8,128)(2,1)S(1)}, u32[]{:S(2)}, u32[]{:S(2)}) async-start(bf16[64,12,384]{2,0,1:T(8,128)(2,1)} %bitcast.63), calls=%async_computation.1 | async-start | bytes 1179648 | tf_op jit(solution)/shard_map/all_to_all | solution.py:28
  100.3 37.8 %all-gather.1 = f32[64,1,3]{2,1,0:T(1,128)} all-gather(f32[1,1,3]{2,1,0:T(1,128)S(1)} %bitcast.87), channel_id=1, replica_groups=mesh['ctx'=64,'inner'=12] {'ctx'}, dimensions={0}, use_global_device_ids=true | all-gather | bytes 780 | tf_op jit(solution)/shard_map/all_gather | solution.py:11
  138.3 4.6 %fusion.10 = f32[768,3,128]{0,2,1:T(8,128)S(1)} fusion(f32[3,768]{1,0:T(4,128)} %bitcast.85, pred[768,768]{1,0:T(8,128)(4,1)} %iota_compare_fusion, bf16[768,3,128]{2,1,0:T(4,128)(2,1)S(1)} %reshape.99, bf16[768,3,128]{2,1,0:T(4,128)(2,1)} %reshape.97, bf16[768,3,128]{2,1,0:T(4,128)(2,1)S(1)} %reshape.98), kind=kOutput, calls=%fused_computation.17 | convolution fusion | flops 914817024 | bytes 3548160 | tf_op jit(solution)/shard_map/hts,shd->thd/dot_general | solution.py:83
  142.9 47.1 %all-gather.4.cloned.1.call-done = f32[192,128,128]{2,1,0:T(8,128)} async-done(((f32[3,128,128]{2,1,0:T(8,128)}), f32[192,128,128]{2,1,0:T(8,128)}) %all-gather.4.cloned.1.call-update) | async-done | bytes 12582928 | tf_op jit(solution)/shard_map/all_gather | solution.py:11
  190.1 108.5 %while.14 = (s32[]{:T(128)}, f32[3,128,128]{2,1,0:T(8,128)S(1)}, s32[]{:T(128)}, f32[64,3]{1,0:T(8,128)}, f32[64,3,128,128]{3,2,1,0:T(8,128)}, /*index=5*/s32[]{:T(128)}, s32[]{:T(128)}) while((s32[]{:T(128)}, f32[3,128,128]{2,1,0:T(8,128)S(1)}, s32[]{:T(128)}, f32[64,3]{1,0:T(8,128)}, f32[64,3,128,128]{3,2,1,0:T(8,128)}, ...), condition=%wide.region_3.4_spmd.clone, body=%wide.region_2.3_spmd.clone.sunk | while | flops 196612 | bytes 589965 | solution.py:20
  190.8 1.0 fusion.33
  192.5 1.0 fusion.33
  194.2 1.0 fusion.33
  195.9 1.0 fusion.33
  197.7 1.0 fusion.33
  199.4 1.0 fusion.33
  201.1 1.0 fusion.33
  202.8 1.0 fusion.33
  300.1 37.3 %all_to_all.80 = bf16[12,64,384]{2,1,0:T(8,128)(2,1)S(1)} all-to-all(bf16[12,64,384]{2,1,0:T(8,128)(2,1)S(1)} %all_to_all.71), channel_id=1, replica_groups=mesh['ctx'=64,'inner'=12] {'inner'}, dimensions={0} | all-to-all | bytes 1179648 | tf_op jit(solution)/shard_map/all_to_all | solution.py:90
  338.2 1.1 multiply_convert_fusion.1
  (167 shorter events, 110.9 us)
Async XLA Ops:
  6.5 17.2 %copy-start = (bf16[64,32]{0,1:T(8,128)(2,1)S(1)}, bf16[64,32]{0,1:T(8,128)(2,1)}, u32[]{:S(2)}) copy-start(bf16[64,32]{0,1:T(8,128)(2,1)} %param.10) | copy-start | bytes 12292
  7.9 25.3 %all-to-all-start.3 = ((bf16[64,12,3]{0,2,1:T(4,128)(2,1)}), bf16[64,12,3]{0,2,1:T(4,128)(2,1)S(1)}, u32[]{:S(2)}, u32[]{:S(2)}) async-start(bf16[64,12,3]{0,2,1:T(4,128)(2,1)} %all_to_all.69), calls=%async_computation.3 | async-start | bytes 24576 | tf_op jit(solution)/shard_map/all_to_all | solution.py:57
  25.2 11.6 %copy-start.1 = (bf16[32,13824]{1,0:T(8,128)(2,1)S(1)}, bf16[32,13824]{1,0:T(8,128)(2,1)}, u32[]{:S(2)}) copy-start(bf16[32,13824]{1,0:T(8,128)(2,1)} %param.14) | copy-start | bytes 2654212
  25.2 11.5 %copy-start.3 = (bf16[64,4608]{1,0:T(8,128)(2,1)S(1)}, bf16[64,4608]{1,0:T(8,128)(2,1)}, u32[]{:S(2)}) copy-start(bf16[64,4608]{1,0:T(8,128)(2,1)} %param.13) | copy-start | bytes 1769476
  33.1 30.0 %all-to-all-start.2 = ((bf16[64,12,384]{2,0,1:T(8,128)(2,1)}), bf16[64,12,384]{2,0,1:T(8,128)(2,1)S(1)}, u32[]{:S(2)}, u32[]{:S(2)}) async-start(bf16[64,12,384]{2,0,1:T(8,128)(2,1)} %bitcast.62), calls=%async_computation.2 | async-start | bytes 1179648 | tf_op jit(solution)/shard_map/all_to_all | solution.py:56
  63.1 27.4 %all-to-all-start = ((bf16[64,12,384]{2,0,1:T(8,128)(2,1)}), bf16[64,12,384]{2,0,1:T(8,128)(2,1)S(1)}, u32[]{:S(2)}, u32[]{:S(2)}) async-start(bf16[64,12,384]{2,0,1:T(8,128)(2,1)} %bitcast.64), calls=%async_computation | async-start | bytes 1179648 | tf_op jit(solution)/shard_map/all_to_all | solution.py:28
  66.7 123.3 %all-gather.4.cloned.1.call-start = ((), (), s32[]{:S(2)}) async-start(), calls=%async_computation.5 | async-start | bytes 12779520 | tf_op jit(solution)/shard_map/all_gather | solution.py:11
  68.2 0.8 copy-start.7
  91.5 1.1 copy-start.2
  92.7 1.1 copy-start.4
  95.0 43.1 %all-to-all-start.1 = ((bf16[64,12,384]{2,0,1:T(8,128)(2,1)}), bf16[64,12,384]{2,0,1:T(8,128)(2,1)S(1)}, u32[]{:S(2)}, u32[]{:S(2)}) async-start(bf16[64,12,384]{2,0,1:T(8,128)(2,1)} %bitcast.63), calls=%async_computation.1 | async-start | bytes 1179648 | tf_op jit(solution)/shard_map/all_to_all | solution.py:28
  190.1 108.5 %copy-start.5 = (f32[768,3]{0,1:T(4,128)S(1)}, f32[768,3]{0,1:T(4,128)}, u32[]{:S(2)}) copy-start(f32[768,3]{0,1:T(4,128)} %get-tuple-element.131) | copy-start | bytes 27652
  337.4 0.7 copy-start.6
Sparse Core Ops, SparseCore 0:
  93.9 96.1 all-gather.3
where the time goes:
time: 350 us; the launch traced here: 346 us
  waiting for transfers between devices  100 us (29%)
  blocking collectives  75.1 us (21%)
  other arithmetic  69.2 us (20%)
  local copies, waits for them, and re-layouts  51.1 us (15%)
  starting transfers between devices  26.7 us (8%)
  between operations  14.3 us (4%)
  matrix products  8.21 us (2%)
    select_n x63, other arithmetic, hop(): jnp.where(position < mine, new, old)  64.1 us
    all_gather x1, waiting for transfers between devices, carried_in(): pieces = jax.tree.map(lambda part: lax.all_gather(part, axis), value)  47.1 us
    mul x63, local copies, waits for them, and re-layouts, combine(): later[0][:, None, None] * earlier[1] + later[1]  43.3 us
    all_gather x1, blocking collectives, carried_in(): pieces = jax.tree.map(lambda part: lax.all_gather(part, axis), value)  37.8 us
    all_to_all x1, blocking collectives, shards(): lax.all_to_all(mixed_out, 'inner', split_axis=0, concat_axis=1, tiled=True)  37.3 us
    all_to_all x1, waiting for transfers between devices, shards(): lax.all_to_all(keys_all, 'inner', split_axis=1, concat_axis=0, tiled=True)  25.1 us
    all_to_all x2, waiting for transfers between devices, rows_to_heads(): lax.all_to_all(rows, 'inner', split_axis=1, concat_axis=0, tiled=True)  21.1 us
    all_to_all x1, starting transfers between devices, shards(): lax.all_to_all(log_decay, 'inner', split_axis=1, concat_axis=0, tiled=True)  15.2 us
  transfers between devices with their start and end apart: 5, of which 4 were waited for; matrix products, arithmetic and copies ran while one was open for 4% of the time, Pallas kernels for 0%

commit v1 on v0

v1 whole, which is shorter than its diff:
```python
import functools

import jax
import jax.numpy as jnp
from jax import lax
from jax.experimental import pallas as pl
from jax.experimental.pallas import tpu as pltpu
from jax.sharding import PartitionSpec as P

MESH = pl.DeviceIdType.MESH
F32 = jnp.float32
BF16 = jnp.bfloat16
GROUP = 16
STRIDE = 3


def across(a, b, left, right):
    return lax.dot_general(a, b, (((left,), (right,)), ((), ())), preferred_element_type=F32)


def kernel(
    sizes,
    lr_ref, q_hbm, k_hbm, v_hbm, up_hbm, ld_ref, gain_ref, len_ref,
    out_ref,
    qv, kv, vv, up, dbc, drow, st, esend, ebuf, cols,
    ms_s, ms_r, ps_s, ps_r, ch_s, ch_r,
    c_s, c_r, pre, cum, f_s, f_r, x_s, x_r, ag, oac, gac,
    in_sem, es_sem, er_sem, rs_sem, rr_sem, chs_sem, chr_sem,
    cs_sem, cr_sem, fs_sem, fr_sem, xs_sem, xr_sem, as_sem, ar_sem,
):
    zn, group, nx, heads, hp, rows, dh = sizes
    nm = zn // 2
    np_ = zn - 1 - nm
    wide = heads * dh
    slab = dh // group
    z = lax.axis_index("inner")
    c = lax.axis_index("ctx")
    r = lax.rem(c, group)
    x = c // group
    up_z = lax.rem(z + 1, zn)
    down_z = lax.rem(z + zn - 1, zn)

    def owner_of(shift):
        return lax.rem(z + shift + zn, zn)

    def send(src, dst, s_sem, r_sem, where):
        copy = pltpu.make_async_remote_copy(
            src_ref=src, dst_ref=dst, send_sem=s_sem, recv_sem=r_sem,
            device_id=where, device_id_type=MESH,
        )
        return copy

    loads = [
        pltpu.make_async_copy(src, dst, in_sem.at[i])
        for i, (src, dst) in enumerate(((k_hbm, kv), (v_hbm, vv), (up_hbm, up), (q_hbm, qv)))
    ]
    for load in loads:
        load.start()

    barrier = pltpu.get_barrier_semaphore()

    def greet_z(i, carry):
        pl.semaphore_signal(
            barrier, inc=1, device_id={"inner": lax.rem(z + i, zn)}, device_id_type=MESH
        )
        return carry

    def greet_r(i, carry):
        pl.semaphore_signal(
            barrier, inc=1, device_id={"ctx": x * group + lax.rem(r + i, group)},
            device_id_type=MESH,
        )
        return carry

    def greet_x(i, carry):
        pl.semaphore_signal(
            barrier, inc=1, device_id={"ctx": lax.rem(x + i, nx) * group + r},
            device_id_type=MESH,
        )
        return carry

    lax.fori_loop(1, zn, greet_z, 0)
    lax.fori_loop(1, group, greet_r, 0)
    lax.fori_loop(1, nx, greet_x, 0)

    ld = ld_ref[...]
    row_i = lax.broadcasted_iota(jnp.int32, (rows, rows), 0)
    col_i = lax.broadcasted_iota(jnp.int32, (rows, rows), 1)
    causal = row_i >= col_i
    tri = causal.astype(F32).astype(BF16)
    triu = (row_i <= col_i).astype(F32).astype(BF16)
    drow[...] = jnp.dot(ld, triu, preferred_element_type=F32)
    lane_head = lax.broadcasted_iota(jnp.int32, (heads, dh), 1)
    pick = (lane_head == lax.broadcasted_iota(jnp.int32, (heads, dh), 0)).astype(F32).astype(BF16)
    per_head = across(ld, pick, 0, 0).astype(BF16)
    esend[...] = jnp.dot(jnp.ones((8, rows), BF16), per_head, preferred_element_type=F32)[0:1]
    ebuf[z] = esend[...]

    pl.semaphore_wait(barrier, (zn - 1) + (group - 1) + (nx - 1))

    def send_e(i, carry):
        to = lax.rem(z + i, zn)
        send(esend, ebuf.at[z], es_sem.at[i], er_sem.at[z], {"inner": to}).start()
        return carry

    lax.fori_loop(1, zn, send_e, 0)

    def decay_cols(o, carry):
        lane = lax.broadcasted_iota(jnp.int32, (heads, hp * dh), 1)
        head = lax.broadcasted_iota(jnp.int32, (heads, hp * dh), 0)
        low = (head - o * hp) * dh
        sel = ((lane >= low) & (lane < low + dh)).astype(F32).astype(BF16)
        spread = across(ld, sel, 0, 0).astype(BF16)
        at = pl.ds(pl.multiple_of(o * hp * dh, hp * dh), hp * dh)
        dbc[:, at] = jnp.dot(tri, spread, preferred_element_type=F32)
        return carry

    lax.fori_loop(0, zn, decay_cols, 0, unroll=2)

    length = len_ref[0]
    live = (lax.broadcasted_iota(jnp.int32, (rows, 1), 0) + z * rows) < length
    lr = lr_ref[...]
    for load in loads[:3]:
        load.wait()

    def chunk_state(o, carry):
        at = pl.ds(pl.multiple_of(o * hp * dh, hp * dh), hp * dh)
        at_k = pl.ds(pl.multiple_of(wide + o * hp * dh, hp * dh), hp * dh)
        at_v = pl.ds(pl.multiple_of(2 * wide + o * hp * dh, hp * dh), hp * dh)
        kb = jnp.where(live, kv[:, at].astype(F32) + across(lr, up[:, at_k], 0, 0), 0.0)
        vb = jnp.where(live, vv[:, at].astype(F32) + across(lr, up[:, at_v], 0, 0), 0.0)
        kb = kb.astype(BF16)
        vb = vb.astype(BF16)
        kv[:, at] = kb
        vv[:, at] = vb
        d = dbc[:, at]
        scaled = (kb.astype(F32) * jnp.exp(d[rows - 1 :, :] - d)).astype(BF16)
        for k in range(hp):
            span = slice(k * dh, (k + 1) * dh)
            st[o * hp + k] = across(scaled[:, span], vb[:, span], 0, 0)
        return carry

    lax.fori_loop(0, zn, chunk_state, 0, unroll=2)

    loads[3].wait()

    def edit_q(o, carry):
        at = pl.ds(pl.multiple_of(o * hp * dh, hp * dh), hp * dh)
        qv[:, at] = (qv[:, at].astype(F32) + across(lr, up[:, at], 0, 0)).astype(BF16)
        return carry

    lax.fori_loop(0, zn, edit_q, 0, unroll=2)

    @pl.when(z == 0)
    def _():
        ch_r[...] = jnp.zeros_like(ch_r)

    def wait_e(i, carry):
        src = lax.rem(z + i, zn)
        send(esend, ebuf.at[src], es_sem.at[i], er_sem.at[src], {"inner": src}).wait_recv()
        return carry

    lax.fori_loop(1, zn, wait_e, 0)
    before = jnp.zeros((1, dh), F32)
    after = jnp.zeros((1, dh), F32)
    whole = jnp.zeros((1, dh), F32)
    for i in range(zn):
        e_i = ebuf[i]
        before = before + jnp.where(z > i, e_i, 0.0)
        after = after + jnp.where(z < i, e_i, 0.0)
        whole = whole + e_i
    eye = lax.broadcasted_iota(jnp.int32, (dh, dh), 0) == lax.broadcasted_iota(
        jnp.int32, (dh, dh), 1
    )
    for i, vec in enumerate((esend[...], after, before, whole)):
        column = jnp.sum(jnp.where(eye, vec, 0.0), axis=1, keepdims=True)
        cols[i] = jnp.broadcast_to(jnp.exp(column), (dh, dh))

    def factor(kind, head):
        return cols[kind, pl.ds(head, 1), :]

    def chain_head(h):
        @pl.when(z > 0)
        def _():
            send(
                ch_s.at[h], ch_r.at[h], chs_sem.at[h], chr_sem.at[h], {"inner": up_z}
            ).wait_recv()

        prior = ch_r[h]

        @pl.when(z < zn - 1)
        def _():
            ch_s[h] = (prior.astype(F32) * factor(0, h) + st[h]).astype(BF16)
            send(
                ch_s.at[h], ch_r.at[h], chs_sem.at[h], chr_sem.at[h], {"inner": up_z}
            ).start()

        at = pl.ds(pl.multiple_of(h * dh, dh), dh)
        qh = qv[:, at]
        d = dbc[:, at]
        scores = across(qh, kv[:, at], 1, 1)
        gap = d[:, 0:rows] - drow[pl.ds(h, 1), :]
        weights = jnp.where(causal, scores * jnp.exp(jnp.where(causal, gap, 0.0)), 0.0)
        oac[:, at] = jnp.dot(
            weights.astype(BF16), vv[:, at], preferred_element_type=F32
        ) + jnp.exp(d) * jnp.dot(qh, prior, preferred_element_type=F32)

    total_steps = heads + STRIDE * (zn - 1)

    def chain(first, last):
        def step(n, carry):
            h = n - STRIDE * z

            @pl.when((h >= 0) & (h < heads))
            def _():
                chain_head(h)

            return carry

        lax.fori_loop(min(first, total_steps), min(last, total_steps), step, 0)

    def minus_copy(s, k):
        return send(
            ms_s.at[s, k], ms_r.at[s, k], rs_sem.at[s, k], rr_sem.at[s, k], {"inner": down_z}
        )

    def plus_copy(s, k):
        return send(
            ps_s.at[s, k], ps_r.at[s, k], rs_sem.at[nm + s, k], rr_sem.at[nm + s, k],
            {"inner": up_z},
        )

    done = 0
    for s in range(nm):
        o = owner_of(s - nm)
        for k in range(hp):
            h = o * hp + k
            part = st[h] * factor(1, h)
            if s:
                minus_copy(s - 1, k).wait_recv()
                part = part + ms_r[s - 1, k].astype(F32)
            ms_s[s, k] = part.astype(BF16)
            minus_copy(s, k).start()
        if s < np_:
            o = owner_of(np_ - s)
            for k in range(hp):
                h = o * hp + k
                part = st[h] * factor(1, h)
                if s:
                    plus_copy(s - 1, k).wait_recv()
                    part = part + ps_r[s - 1, k].astype(F32)
                ps_s[s, k] = part.astype(BF16)
                plus_copy(s, k).start()
        chain(done, done + 3)
        done += 3

    tile_row = lax.broadcasted_iota(jnp.int32, (slab, dh), 0)
    decay_tile = jnp.zeros((slab, dh), F32)
    for k in range(hp):
        h = z * hp + k
        minus_copy(nm - 1, k).wait_recv()
        plus_copy(np_ - 1, k).wait_recv()
        part = st[h] * factor(1, h) + ms_r[nm - 1, k].astype(F32) + ps_r[np_ - 1, k].astype(F32)
        c_s[:, k] = part.reshape(group, slab, dh)
        decay_tile = jnp.where(tile_row == k, factor(3, h), decay_tile)
    c_s[:, hp] = jnp.broadcast_to(decay_tile[None], (group, slab, dh))

    def c_copy(peer, slot):
        return send(
            c_s.at[peer], c_r.at[slot], cs_sem.at[peer], cr_sem.at[slot],
            {"ctx": x * group + peer},
        )

    def f_copy(peer, slot):
        return send(
            f_s.at[peer], f_r.at[slot], fs_sem.at[peer], fr_sem.at[slot],
            {"ctx": x * group + peer},
        )

    def x_copy(i, peer, slot):
        return send(
            x_s, x_r.at[slot], xs_sem.at[i], xr_sem.at[slot], {"ctx": peer * group + r}
        )

    def start_c(i, carry):
        c_copy(lax.rem(r + i, group), r).start()
        return carry

    def wait_c(i, carry):
        peer = lax.rem(r + i, group)
        c_copy(peer, peer).wait_recv()
        return carry

    lax.fori_loop(1, group, start_c, 0)
    c_r[r] = c_s[r]
    chain(done, done + 12)
    done += 12
    lax.fori_loop(1, group, wait_c, 0)

    carry_state = [jnp.zeros((slab, dh), F32) for _ in range(hp)]
    carry_decay = [jnp.ones((1, dh), F32) for _ in range(hp)]
    for i in range(group):
        tile = c_r[i, hp]
        for k in range(hp):
            here = tile[k : k + 1]
            pre[i, k] = carry_state[k]
            cum[i, k] = jnp.broadcast_to(carry_decay[k], (slab, dh))
            carry_state[k] = here * carry_state[k] + c_r[i, k]
            carry_decay[k] = here * carry_decay[k]
    for k in range(hp):
        x_s[k] = carry_state[k]
        x_s[hp + k] = jnp.broadcast_to(carry_decay[k], (slab, dh))

    def start_x(i, carry):
        x_copy(i, lax.rem(x + i, nx), x).start()
        return carry

    def wait_x(i, carry):
        peer = lax.rem(x + i, nx)
        x_copy(i, peer, peer).wait_recv()
        return carry

    lax.fori_loop(1, nx, start_x, 0)
    x_r[x] = x_s[...]
    chain(done, done + 5)
    done += 5
    lax.fori_loop(1, nx, wait_x, 0)
    for k in range(hp):
        entry = jnp.zeros((slab, dh), F32)
        for i in range(nx):
            entry = jnp.where(x > i, x_r[i, hp + k] * entry + x_r[i, k], entry)
        f_s[:, k] = pre[:, k] + cum[:, k] * entry[None]

    def start_f(i, carry):
        f_copy(lax.rem(r + i, group), r).start()
        return carry

    def wait_f(i, carry):
        peer = lax.rem(r + i, group)
        f_copy(peer, peer).wait_recv()
        return carry

    lax.fori_loop(1, group, start_f, 0)
    f_r[r] = f_s[r]
    chain(done, done + 11)
    done += 11
    lax.fori_loop(1, group, wait_f, 0)
    for k in range(hp):
        ag[z, k] = f_r[:, k].reshape(dh, dh).astype(BF16)

    def ag_minus(s, o, k):
        return send(
            ag.at[o, k], ag.at[o, k], as_sem.at[s, k], ar_sem.at[s, k], {"inner": down_z}
        )

    def ag_plus(s, o, k):
        return send(
            ag.at[o, k], ag.at[o, k], as_sem.at[nm + s, k], ar_sem.at[nm + s, k],
            {"inner": up_z},
        )

    def former_term(o):
        for k in range(hp):
            h = o * hp + k
            at = pl.ds(pl.multiple_of(h * dh, dh), dh)
            inter = jnp.dot(qv[:, at], ag[o, k], preferred_element_type=F32)
            gac[:, at] = jnp.exp(dbc[:, at]) * factor(2, h) * inter

    for k in range(hp):
        ag_minus(0, z, k).start()
        ag_plus(0, z, k).start()
    former_term(z)
    rest = -(-max(total_steps - done, 0) // nm)
    for s in range(nm):
        o_m = owner_of(s + 1)
        o_p = owner_of(-1 - s)
        for k in range(hp):
            ag_minus(s, o_m, k).wait_recv()
            if s + 1 < nm:
                ag_minus(s + 1, o_m, k).start()
        if s < np_:
            for k in range(hp):
                ag_plus(s, o_p, k).wait_recv()
                if s + 1 < np_:
                    ag_plus(s + 1, o_p, k).start()
        former_term(o_m)
        if s < np_:
            former_term(o_p)
        chain(done, done + rest)
        done += rest

    def mix(h, acc):
        at = pl.ds(pl.multiple_of(h * dh, dh), dh)
        mixed = jnp.where(live, oac[:, at] + gac[:, at], 0.0).astype(BF16)
        qv[:, at] = mixed
        wide_mixed = mixed.astype(F32)
        return acc + wide_mixed * wide_mixed

    acc = lax.fori_loop(0, heads, mix, jnp.zeros((rows, dh), F32), unroll=4)
    mean = jnp.sum(acc, axis=1, keepdims=True) / wide
    inv = lax.rsqrt(mean + 1e-6)

    def scale(o, carry):
        at = pl.ds(pl.multiple_of(o * hp * dh, hp * dh), hp * dh)
        out_ref[:, at] = (qv[:, at].astype(F32) * inv * gain_ref[:, at]).astype(BF16)
        return carry

    lax.fori_loop(0, zn, scale, 0, unroll=2)

    def left_e(i, carry):
        to = lax.rem(z + i, zn)
        send(esend, ebuf.at[z], es_sem.at[i], er_sem.at[z], {"inner": to}).wait_send()
        return carry

    lax.fori_loop(1, zn, left_e, 0)
    for s in range(nm):
        for k in range(hp):
            minus_copy(s, k).wait_send()
            ag_minus(s, owner_of(s), k).wait_send()
    for s in range(np_):
        for k in range(hp):
            plus_copy(s, k).wait_send()
            ag_plus(s, owner_of(-s), k).wait_send()

    def left_r(i, carry):
        peer = lax.rem(r + i, group)
        c_copy(peer, r).wait_send()
        f_copy(peer, r).wait_send()
        return carry

    lax.fori_loop(1, group, left_r, 0)

    def left_x(i, carry):
        x_copy(i, lax.rem(x + i, nx), x).wait_send()
        return carry

    lax.fori_loop(1, nx, left_x, 0)

    @pl.when(z < zn - 1)
    def _():
        def left_ch(h, carry):
            send(
                ch_s.at[h], ch_r.at[h], chs_sem.at[h], chr_sem.at[h], {"inner": up_z}
            ).wait_send()
            return carry

        lax.fori_loop(0, heads, left_ch, 0)


def shards(low_rank, q_base, k_base, v_base, edit_up, log_decay, lengths, norm_gain):
    rows, wide = q_base.shape
    rank = low_rank.shape[1]
    heads = log_decay.shape[1]
    dh = wide // heads
    zn = lax.axis_size("inner")
    ctx = lax.axis_size("ctx")
    group = GROUP
    nx = ctx // group
    hp = heads // zn
    nm = zn // 2
    np_ = zn - 1 - nm
    slab = dh // group
    sizes = (zn, group, nx, heads, hp, rows, dh)
    vmem = pl.BlockSpec(memory_space=pltpu.VMEM)
    anywhere = pl.BlockSpec(memory_space=pl.ANY)
    dma = pltpu.SemaphoreType.DMA
    call = pl.pallas_call(
        functools.partial(kernel, sizes),
        out_shape=jax.ShapeDtypeStruct((rows, wide), BF16),
        in_specs=[
            vmem, anywhere, anywhere, anywhere, anywhere, vmem, vmem,
            pl.BlockSpec(memory_space=pltpu.SMEM),
        ],
        out_specs=vmem,
        scratch_shapes=[
            pltpu.VMEM((rows, wide), BF16),
            pltpu.VMEM((rows, wide), BF16),
            pltpu.VMEM((rows, wide), BF16),
            pltpu.VMEM((rank, 3 * wide), BF16),
            pltpu.VMEM((rows, wide), F32),
            pltpu.VMEM((heads, rows), F32),
            pltpu.VMEM((heads, dh, dh), F32),
            pltpu.VMEM((1, dh), F32),
            pltpu.VMEM((zn, 1, dh), F32),
            pltpu.VMEM((4, dh, dh), F32),
            pltpu.VMEM((nm, hp, dh, dh), BF16),
            pltpu.VMEM((nm, hp, dh, dh), BF16),
            pltpu.VMEM((np_, hp, dh, dh), BF16),
            pltpu.VMEM((np_, hp, dh, dh), BF16),
            pltpu.VMEM((heads, dh, dh), BF16),
            pltpu.VMEM((heads, dh, dh), BF16),
            pltpu.VMEM((group, hp + 1, slab, dh), F32),
            pltpu.VMEM((group, hp + 1, slab, dh), F32),
            pltpu.VMEM((group, hp, slab, dh), F32),
            pltpu.VMEM((group, hp, slab, dh), F32),
            pltpu.VMEM((group, hp, slab, dh), F32),
            pltpu.VMEM((group, hp, slab, dh), F32),
            pltpu.VMEM((2 * hp, slab, dh), F32),
            pltpu.VMEM((nx, 2 * hp, slab, dh), F32),
            pltpu.VMEM((zn, hp, dh, dh), BF16),
            pltpu.VMEM((rows, wide), F32),
            pltpu.VMEM((rows, wide), F32),
            dma((4,)),
            dma((zn,)), dma((zn,)),
            dma((nm + np_, hp)), dma((nm + np_, hp)),
            dma((heads,)), dma((heads,)),
            dma((group,)), dma((group,)),
            dma((group,)), dma((group,)),
            dma((nx,)), dma((nx,)),
            dma((nm + np_, hp)), dma((nm + np_, hp)),
        ],
        compiler_params=pltpu.CompilerParams(
            collective_id=0, has_side_effects=True, vmem_limit_bytes=60 * 1024 * 1024
        ),
    )
    return call(
        low_rank.T, q_base, k_base, v_base, edit_up, log_decay.T,
        norm_gain.reshape(1, wide), lengths,
    )


def solution(mesh):
    rows = P(("ctx", "inner"), None)
    return jax.shard_map(
        shards,
        mesh=mesh,
        in_specs=(rows, rows, rows, rows, P(), rows, P("ctx"), P()),
        out_specs=rows,
        check_vma=False,
    )
```

time: 350 us -> 114 us (0.33)
  the two profiles are of different devices: /device:TPU:8 before, /device:TPU:4 now
where the time goes in v1:
time: 114 us; the launch traced here: 113 us
  Pallas kernels  110 us (96%)
  local copies, waits for them, and re-layouts  3.26 us (3%)
    pallas_call x1, Pallas kernels, shards(): call(low_rank.T, q_base, k_base, v_base, edit_up, log_decay.T, norm_gain....  110 us

profile of v1, /device:TPU:4, one launch (start us, length us, event | category | flops | bytes accessed | tf_op | source)
XLA Modules:
  0.0 113.4 jit_solution(16807956402468426624)
XLA Ops:
  0.7 1.3 %reshape.3.gain_ref = f32[1,4608]{1,0:T(1,128)} reshape(f32[4608]{0:T(1024)} %param.15) | data formatting | bytes 36864 | tf_op jit(solution)/shard_map/reshape | solution.py:518
  2.0 109.5 %shard_map.82 = bf16[64,4608]{1,0:T(8,128)(2,1)} custom-call(bf16[32,64]{1,0:T(8,128)(2,1)} %bitcast.3, bf16[64,4608]{1,0:T(8,128)(2,1)} %q_hbm.1, bf16[64,4608]{1,0:T(8,128)(2,1)} %k_hbm.1, bf16[64,4608]{1,0:T(8,128)(2,1)} %v_hbm.1, bf16[32,13824]{1,0:T(8,128)(2,1)} %up_hbm.1, bf16[36,64]{1,0:T(8,128)(2,1)} %bitcast.2, f32[1,4608]{1,0:T(1,128)} %reshape.3.gain_ref, ...), custom_call_target="tpu_custom_call" | custom-call | tf_op jit(solution)/shard_map/pallas_call | solution.py:516
  111.5 1.9 %copy.11 = bf16[64,4608]{1,0:T(8,128)(2,1)} copy(bf16[64,4608]{1,0:T(8,128)(2,1)} %shard_map.82) | data formatting | bytes 1179648

commit v2 on v1

v2 whole, which is shorter than its diff:
```python
import functools

import jax
import jax.numpy as jnp
from jax import lax
from jax.experimental import pallas as pl
from jax.experimental.pallas import tpu as pltpu
from jax.sharding import PartitionSpec as P

MESH = pl.DeviceIdType.MESH
F32 = jnp.float32
BF16 = jnp.bfloat16
GROUP = 16
STRIDE = 4
EARLY = True
REDUCE_MINUS = 6
GATHER_MINUS = 6
REDUCE_STEPS = (1, 1, 1)
GATHER_STEPS = (1, 2, 1)
UNITS = (8, 11)
C_STEPS = (1, 1, 1, 1)
P_STEPS = 24


def split_of(zn, minus):
    minus = min(max(minus, zn // 2), zn - 2)
    return minus, zn - 1 - minus


def across(a, b, left, right):
    return lax.dot_general(a, b, (((left,), (right,)), ((), ())), preferred_element_type=F32)


def kernel(
    sizes,
    lr_ref, q_hbm, k_hbm, v_hbm, up_hbm, ld_ref, gain_ref, len_ref,
    out_ref,
    qv, kv, vv, up, dbc, drow, st, esend, ebuf, cols,
    ms_s, ms_r, ps_s, ps_r, ch_s, ch_r,
    c_s, c_r, pre, cum, f_s, f_r, x_s, x_r, ag, oac, gac,
    in_sem, es_sem, er_sem, rs_sem, rr_sem, chs_sem, chr_sem,
    cs_sem, cr_sem, fs_sem, fr_sem, xs_sem, xr_sem, as_sem, ar_sem,
):
    zn, group, nx, heads, hp, rows, dh = sizes
    rm, rp = split_of(zn, REDUCE_MINUS)
    am, ap = split_of(zn, GATHER_MINUS)
    wide = heads * dh
    slab = dh // group
    z = lax.axis_index("inner")
    c = lax.axis_index("ctx")
    r = lax.rem(c, group)
    x = c // group
    up_z = lax.rem(z + 1, zn)
    down_z = lax.rem(z + zn - 1, zn)

    def owner_of(shift):
        return lax.rem(z + shift + zn, zn)

    def send(src, dst, s_sem, r_sem, where):
        copy = pltpu.make_async_remote_copy(
            src_ref=src, dst_ref=dst, send_sem=s_sem, recv_sem=r_sem,
            device_id=where, device_id_type=MESH,
        )
        return copy

    loads = [
        pltpu.make_async_copy(src, dst, in_sem.at[i])
        for i, (src, dst) in enumerate(((k_hbm, kv), (v_hbm, vv), (up_hbm, up), (q_hbm, qv)))
    ]
    for load in loads:
        load.start()

    barrier = pltpu.get_barrier_semaphore()

    def greet_z(i, carry):
        pl.semaphore_signal(
            barrier, inc=1, device_id={"inner": lax.rem(z + i, zn)}, device_id_type=MESH
        )
        return carry

    def greet_r(i, carry):
        pl.semaphore_signal(
            barrier, inc=1, device_id={"ctx": x * group + lax.rem(r + i, group)},
            device_id_type=MESH,
        )
        return carry

    def greet_x(i, carry):
        pl.semaphore_signal(
            barrier, inc=1, device_id={"ctx": lax.rem(x + i, nx) * group + r},
            device_id_type=MESH,
        )
        return carry

    lax.fori_loop(1, zn, greet_z, 0)
    lax.fori_loop(1, group, greet_r, 0)
    lax.fori_loop(1, nx, greet_x, 0)

    ld = ld_ref[...]
    row_i = lax.broadcasted_iota(jnp.int32, (rows, rows), 0)
    col_i = lax.broadcasted_iota(jnp.int32, (rows, rows), 1)
    causal = row_i >= col_i
    tri = causal.astype(F32).astype(BF16)
    triu = (row_i <= col_i).astype(F32).astype(BF16)
    drow[...] = jnp.dot(ld, triu, preferred_element_type=F32)
    lane_head = lax.broadcasted_iota(jnp.int32, (heads, dh), 1)
    pick = (lane_head == lax.broadcasted_iota(jnp.int32, (heads, dh), 0)).astype(F32).astype(BF16)
    per_head = across(ld, pick, 0, 0).astype(BF16)
    esend[...] = jnp.dot(jnp.ones((8, rows), BF16), per_head, preferred_element_type=F32)[0:1]
    ebuf[z] = esend[...]
    eye = lax.broadcasted_iota(jnp.int32, (dh, dh), 0) == lax.broadcasted_iota(
        jnp.int32, (dh, dh), 1
    )

    def keep_exp(kind, vec):
        column = jnp.sum(jnp.where(eye, vec, 0.0), axis=1, keepdims=True)
        cols[kind] = jnp.broadcast_to(jnp.exp(column), (dh, dh))

    def factor(kind, head):
        return cols[kind, pl.ds(head, 1), :]

    keep_exp(0, esend[...])

    def decay_cols(o, carry):
        lane = lax.broadcasted_iota(jnp.int32, (heads, hp * dh), 1)
        head = lax.broadcasted_iota(jnp.int32, (heads, hp * dh), 0)
        low = (head - o * hp) * dh
        sel = ((lane >= low) & (lane < low + dh)).astype(F32).astype(BF16)
        spread = across(ld, sel, 0, 0).astype(BF16)
        at = pl.ds(pl.multiple_of(o * hp * dh, hp * dh), hp * dh)
        dbc[:, at] = jnp.dot(tri, spread, preferred_element_type=F32)
        return carry

    lax.fori_loop(0, zn, decay_cols, 0, unroll=2)

    @pl.when(z == 0)
    def _():
        ch_r[...] = jnp.zeros_like(ch_r)

    pl.semaphore_wait(barrier, (zn - 1) + (group - 1) + (nx - 1))

    def send_e(i, carry):
        to = lax.rem(z + i, zn)
        send(esend, ebuf.at[z], es_sem.at[i], er_sem.at[z], {"inner": to}).start()
        return carry

    lax.fori_loop(1, zn, send_e, 0)

    def chain_copy(h):
        return send(ch_s.at[h], ch_r.at[h], chs_sem.at[h], chr_sem.at[h], {"inner": up_z})

    def chain_head(h):
        @pl.when(z > 0)
        def _():
            chain_copy(h).wait_recv()

        @pl.when(z < zn - 1)
        def _():
            ch_s[h] = (ch_r[h].astype(F32) * factor(0, h) + st[h]).astype(BF16)
            chain_copy(h).start()

    total_steps = heads + STRIDE * (zn - 1)

    def paced(work, first, last):
        def step(n, carry):
            h = n - STRIDE * z

            @pl.when((h >= 0) & (h < heads))
            def _():
                work(h)

            return carry

        first, last = min(first, total_steps), min(last, total_steps)
        if last == first + 1:
            step(first, 0)
        elif last > first:
            lax.fori_loop(first, last, step, 0)

    progress = {"chain": 0, "prior": 0}

    def chain(count):
        paced(chain_head, progress["chain"], progress["chain"] + count)
        progress["chain"] += count

    length = len_ref[0]
    live = (lax.broadcasted_iota(jnp.int32, (rows, 1), 0) + z * rows) < length
    lr = lr_ref[...]
    for load in loads[:3]:
        load.wait()

    def chunk_state(o):
        at = pl.ds(pl.multiple_of(o * hp * dh, hp * dh), hp * dh)
        at_k = pl.ds(pl.multiple_of(wide + o * hp * dh, hp * dh), hp * dh)
        at_v = pl.ds(pl.multiple_of(2 * wide + o * hp * dh, hp * dh), hp * dh)
        kb = jnp.where(live, kv[:, at].astype(F32) + across(lr, up[:, at_k], 0, 0), 0.0)
        vb = jnp.where(live, vv[:, at].astype(F32) + across(lr, up[:, at_v], 0, 0), 0.0)
        kb = kb.astype(BF16)
        vb = vb.astype(BF16)
        kv[:, at] = kb
        vv[:, at] = vb
        d = dbc[:, at]
        scaled = (kb.astype(F32) * jnp.exp(d[rows - 1 :, :] - d)).astype(BF16)
        for k in range(hp):
            span = slice(k * dh, (k + 1) * dh)
            st[o * hp + k] = across(scaled[:, span], vb[:, span], 0, 0)

    pair = 2 if zn % 2 == 0 else 1

    def state_pair(i, carry):
        for j in range(pair):
            chunk_state(pair * i + j)
        if EARLY:
            h = i - STRIDE * z

            @pl.when((h >= 0) & (h < heads))
            def _():
                chain_head(h)

        return carry

    lax.fori_loop(0, zn // pair, state_pair, 0)
    if EARLY:
        progress["chain"] = zn // pair

    def wait_e(i, carry):
        src = lax.rem(z + i, zn)
        send(esend, ebuf.at[src], es_sem.at[i], er_sem.at[src], {"inner": src}).wait_recv()
        return carry

    lax.fori_loop(1, zn, wait_e, 0)
    before = jnp.zeros((1, dh), F32)
    after = jnp.zeros((1, dh), F32)
    whole = jnp.zeros((1, dh), F32)
    for i in range(zn):
        e_i = ebuf[i]
        before = before + jnp.where(z > i, e_i, 0.0)
        after = after + jnp.where(z < i, e_i, 0.0)
        whole = whole + e_i
    keep_exp(1, after)

    def minus_copy(s, k):
        return send(
            ms_s.at[s, k], ms_r.at[s, k], rs_sem.at[s, k], rr_sem.at[s, k], {"inner": down_z}
        )

    def plus_copy(s, k):
        return send(
            ps_s.at[s, k], ps_r.at[s, k], rs_sem.at[rm + s, k], rr_sem.at[rm + s, k],
            {"inner": up_z},
        )

    def reduce_step(copy, out, got, s, o, k):
        h = o * hp + k
        part = st[h] * factor(1, h)
        if s:
            copy(s - 1, k).wait_recv()
            part = part + got[s - 1, k].astype(F32)
        out[s, k] = part.astype(BF16)
        copy(s, k).start()

    for s in range(rm):
        for k in range(hp):
            if s < rp:
                reduce_step(plus_copy, ps_s, ps_r, s, owner_of(rp - s), k)
            reduce_step(minus_copy, ms_s, ms_r, s, owner_of(s - rm), k)
            if s == 0 and k < hp - 1:
                plus_copy(s, k).wait_send()
                minus_copy(s, k).wait_send()
            chain(REDUCE_STEPS[k])
        if s == 0:
            keep_exp(2, before)
            keep_exp(3, whole)

    tile_row = lax.broadcasted_iota(jnp.int32, (slab, dh), 0)
    tile = jnp.zeros((slab, dh), F32)
    for k in range(hp):
        fall = factor(3, z * hp + k)
        high = fall.astype(BF16).astype(F32)
        tile = jnp.where(tile_row == k, high, tile)
        tile = jnp.where(tile_row == k + 4, fall - high, tile)
    parts = []
    for k in range(hp):
        h = z * hp + k
        plus_copy(rp - 1, k).wait_recv()
        minus_copy(rm - 1, k).wait_recv()
        part = st[h] * factor(1, h) + ms_r[rm - 1, k].astype(F32) + ps_r[rp - 1, k].astype(F32)
        parts.append(part.reshape(group, slab, dh))
    parts.append(jnp.broadcast_to(tile[None], (group, slab, dh)))
    c_s[...] = jnp.stack(parts, axis=1).reshape(group, (hp + 1) * slab, dh).astype(BF16)

    def c_copy(peer, slot):
        return send(
            c_s.at[peer], c_r.at[slot], cs_sem.at[peer], cr_sem.at[slot],
            {"ctx": x * group + peer},
        )

    def f_copy(peer, slot):
        return send(
            f_s.at[peer], f_r.at[slot], fs_sem.at[peer], fr_sem.at[slot],
            {"ctx": x * group + peer},
        )

    def x_copy(i, peer, slot):
        return send(
            x_s, x_r.at[slot], xs_sem.at[i], xr_sem.at[slot], {"ctx": peer * group + r}
        )

    def start_c(i, carry):
        c_copy(lax.rem(r + i, group), r).start()
        return carry

    def wait_c(i, carry):
        peer = lax.rem(r + i, group)
        c_copy(peer, peer).wait_recv()
        return carry

    def edit_q(o, carry):
        at = pl.ds(pl.multiple_of(o * hp * dh, hp * dh), hp * dh)
        qv[:, at] = (qv[:, at].astype(F32) + across(lr, up[:, at], 0, 0)).astype(BF16)
        return carry

    def intra(h):
        at = pl.ds(pl.multiple_of(h * dh, dh), dh)
        scores = across(qv[:, at], kv[:, at], 1, 1)
        gap = dbc[:, at][:, 0:rows] - drow[pl.ds(h, 1), :]
        weights = jnp.where(causal, scores * jnp.exp(jnp.where(causal, gap, 0.0)), 0.0)
        oac[:, at] = jnp.dot(weights.astype(BF16), vv[:, at], preferred_element_type=F32)

    units = heads // 2

    def fill(first, last):
        base = progress["chain"] - first

        def unit(u, carry):
            intra(2 * u)
            intra(2 * u + 1)
            h = u + base - STRIDE * z

            @pl.when((h >= 0) & (h < heads))
            def _():
                chain_head(h)

            return carry

        first, last = min(first, units), min(last, units)
        lax.fori_loop(first, last, unit, 0)
        progress["chain"] += last - first

    def prior_term(h):
        at = pl.ds(pl.multiple_of(h * dh, dh), dh)
        inter = jnp.dot(qv[:, at], ch_r[h], preferred_element_type=F32)
        oac[:, at] = oac[:, at] + jnp.exp(dbc[:, at]) * inter

    def prior(count):
        last = min(progress["prior"] + count, progress["chain"])
        paced(prior_term, progress["prior"], last)
        progress["prior"] = last

    lax.fori_loop(1, group, start_c, 0)
    c_r[r] = c_s[r]
    loads[3].wait()
    chain(C_STEPS[0])
    lax.fori_loop(0, zn, edit_q, 0, unroll=2)
    chain(C_STEPS[1])
    fill(0, UNITS[0])
    lax.fori_loop(1, group, wait_c, 0)

    carry_state = [jnp.zeros((slab, dh), F32) for _ in range(hp)]
    carry_decay = [jnp.ones((1, dh), F32) for _ in range(hp)]
    for i in range(group):
        got = c_r[i].astype(F32).reshape(hp + 1, slab, dh)
        for k in range(hp):
            here = got[hp, k : k + 1] + got[hp, k + 4 : k + 5]
            pre[i, k] = carry_state[k]
            cum[i, k] = jnp.broadcast_to(carry_decay[k], (slab, dh))
            carry_state[k] = here * carry_state[k] + got[k]
            carry_decay[k] = here * carry_decay[k]
    tile = jnp.zeros((slab, dh), F32)
    for k in range(hp):
        x_s[k] = carry_state[k]
        tile = jnp.where(tile_row == k, carry_decay[k], tile)
    x_s[hp] = tile

    def start_x(i, carry):
        x_copy(i, lax.rem(x + i, nx), x).start()
        return carry

    def wait_x(i, carry):
        peer = lax.rem(x + i, nx)
        x_copy(i, peer, peer).wait_recv()
        return carry

    lax.fori_loop(1, nx, start_x, 0)
    x_r[x] = x_s[...]
    chain(C_STEPS[2])
    fill(UNITS[0], UNITS[1])
    lax.fori_loop(1, nx, wait_x, 0)
    formers = []
    for k in range(hp):
        entry = jnp.zeros((slab, dh), F32)
        for i in range(nx):
            entry = jnp.where(x > i, x_r[i, hp, k : k + 1] * entry + x_r[i, k], entry)
        formers.append(pre[:, k] + cum[:, k] * entry[None])
    formers.append(jnp.zeros((group, slab, dh), F32))
    f_s[...] = jnp.stack(formers, axis=1).reshape(group, (hp + 1) * slab, dh).astype(BF16)

    def start_f(i, carry):
        f_copy(lax.rem(r + i, group), r).start()
        return carry

    def wait_f(i, carry):
        peer = lax.rem(r + i, group)
        f_copy(peer, peer).wait_recv()
        return carry

    lax.fori_loop(1, group, start_f, 0)
    f_r[r] = f_s[r]
    chain(C_STEPS[3])
    fill(UNITS[1], units)
    prior(P_STEPS)
    lax.fori_loop(1, group, wait_f, 0)
    got = f_r[...].astype(F32).reshape(group, hp + 1, slab, dh)
    for k in range(hp):
        ag[z, k] = got[:, k].reshape(dh, dh).astype(BF16)

    def ag_minus(s, o, k):
        return send(
            ag.at[o, k], ag.at[o, k], as_sem.at[s, k], ar_sem.at[s, k], {"inner": down_z}
        )

    def ag_plus(s, o, k):
        return send(
            ag.at[o, k], ag.at[o, k], as_sem.at[am + s, k], ar_sem.at[am + s, k],
            {"inner": up_z},
        )

    def former_term(o):
        for k in range(hp):
            h = o * hp + k
            at = pl.ds(pl.multiple_of(h * dh, dh), dh)
            inter = jnp.dot(qv[:, at], ag[o, k], preferred_element_type=F32)
            gac[:, at] = jnp.exp(dbc[:, at]) * factor(2, h) * inter

    for k in range(hp):
        ag_plus(0, z, k).start()
        ag_minus(0, z, k).start()
        if k < hp - 1:
            ag_plus(0, z, k).wait_send()
            ag_minus(0, z, k).wait_send()
        chain(GATHER_STEPS[k])
    former_term(z)
    rest_p = -(-max(total_steps - progress["prior"], 0) // am)
    final = am - 1
    for s in range(am):
        o_m = owner_of(s + 1)
        o_p = owner_of(-1 - s)
        for k in range(hp):
            if s < ap:
                ag_plus(s, o_p, k).wait_recv()
                if s + 1 < ap:
                    ag_plus(s + 1, o_p, k).start()
            ag_minus(s, o_m, k).wait_recv()
            if s + 1 < am:
                ag_minus(s + 1, o_m, k).start()
            chain(total_steps if s == final and k + 1 == hp else GATHER_STEPS[k])
        if s < ap:
            former_term(o_p)
        former_term(o_m)
        prior(total_steps if s == final else rest_p)

    def mix(h, acc):
        at = pl.ds(pl.multiple_of(h * dh, dh), dh)
        mixed = jnp.where(live, oac[:, at] + gac[:, at], 0.0).astype(BF16)
        qv[:, at] = mixed
        wide_mixed = mixed.astype(F32)
        return acc + wide_mixed * wide_mixed

    acc = lax.fori_loop(0, heads, mix, jnp.zeros((rows, dh), F32), unroll=4)
    mean = jnp.sum(acc, axis=1, keepdims=True) / wide
    inv = lax.rsqrt(mean + 1e-6)

    def scale(h, carry):
        at = pl.ds(pl.multiple_of(h * dh, dh), dh)
        gain = gain_ref[pl.ds(h, 1), :]
        out_ref[:, at] = (qv[:, at].astype(F32) * inv * gain).astype(BF16)
        return carry

    lax.fori_loop(0, heads, scale, 0, unroll=4)

    def left_e(i, carry):
        to = lax.rem(z + i, zn)
        send(esend, ebuf.at[z], es_sem.at[i], er_sem.at[z], {"inner": to}).wait_send()
        return carry

    lax.fori_loop(1, zn, left_e, 0)
    for k in range(hp):
        first = 0 if k == hp - 1 else 1
        for s in range(first, rm):
            minus_copy(s, k).wait_send()
        for s in range(first, rp):
            plus_copy(s, k).wait_send()
        for s in range(first, am):
            ag_minus(s, owner_of(s), k).wait_send()
        for s in range(first, ap):
            ag_plus(s, owner_of(-s), k).wait_send()

    def left_r(i, carry):
        peer = lax.rem(r + i, group)
        c_copy(peer, r).wait_send()
        f_copy(peer, r).wait_send()
        return carry

    lax.fori_loop(1, group, left_r, 0)

    def left_x(i, carry):
        x_copy(i, lax.rem(x + i, nx), x).wait_send()
        return carry

    lax.fori_loop(1, nx, left_x, 0)

    @pl.when(z < zn - 1)
    def _():
        def left_ch(h, carry):
            chain_copy(h).wait_send()
            return carry

        lax.fori_loop(0, heads, left_ch, 0)


def shards(low_rank, q_base, k_base, v_base, edit_up, log_decay, lengths, norm_gain):
    rows, wide = q_base.shape
    rank = low_rank.shape[1]
    heads = log_decay.shape[1]
    dh = wide // heads
    zn = lax.axis_size("inner")
    ctx = lax.axis_size("ctx")
    group = GROUP
    nx = ctx // group
    hp = heads // zn
    rm, rp = split_of(zn, REDUCE_MINUS)
    slab = dh // group
    sizes = (zn, group, nx, heads, hp, rows, dh)
    vmem = pl.BlockSpec(memory_space=pltpu.VMEM)
    anywhere = pl.BlockSpec(memory_space=pl.ANY)
    dma = pltpu.SemaphoreType.DMA
    call = pl.pallas_call(
        functools.partial(kernel, sizes),
        out_shape=jax.ShapeDtypeStruct((rows, wide), BF16),
        in_specs=[
            vmem, anywhere, anywhere, anywhere, anywhere, vmem, vmem,
            pl.BlockSpec(memory_space=pltpu.SMEM),
        ],
        out_specs=vmem,
        scratch_shapes=[
            pltpu.VMEM((rows, wide), BF16),
            pltpu.VMEM((rows, wide), BF16),
            pltpu.VMEM((rows, wide), BF16),
            pltpu.VMEM((rank, 3 * wide), BF16),
            pltpu.VMEM((rows, wide), F32),
            pltpu.VMEM((heads, rows), F32),
            pltpu.VMEM((heads, dh, dh), F32),
            pltpu.VMEM((1, dh), F32),
            pltpu.VMEM((zn, 1, dh), F32),
            pltpu.VMEM((4, dh, dh), F32),
            pltpu.VMEM((rm, hp, dh, dh), BF16),
            pltpu.VMEM((rm, hp, dh, dh), BF16),
            pltpu.VMEM((rp, hp, dh, dh), BF16),
            pltpu.VMEM((rp, hp, dh, dh), BF16),
            pltpu.VMEM((heads, dh, dh), BF16),
            pltpu.VMEM((heads, dh, dh), BF16),
            pltpu.VMEM((group, (hp + 1) * slab, dh), BF16),
            pltpu.VMEM((group, (hp + 1) * slab, dh), BF16),
            pltpu.VMEM((group, hp, slab, dh), F32),
            pltpu.VMEM((group, hp, slab, dh), F32),
            pltpu.VMEM((group, (hp + 1) * slab, dh), BF16),
            pltpu.VMEM((group, (hp + 1) * slab, dh), BF16),
            pltpu.VMEM((hp + 1, slab, dh), F32),
            pltpu.VMEM((nx, hp + 1, slab, dh), F32),
            pltpu.VMEM((zn, hp, dh, dh), BF16),
            pltpu.VMEM((rows, wide), F32),
            pltpu.VMEM((rows, wide), F32),
            dma((4,)),
            dma((zn,)), dma((zn,)),
            dma((zn - 1, hp)), dma((zn - 1, hp)),
            dma((heads,)), dma((heads,)),
            dma((group,)), dma((group,)),
            dma((group,)), dma((group,)),
            dma((nx,)), dma((nx,)),
            dma((zn - 1, hp)), dma((zn - 1, hp)),
        ],
        compiler_params=pltpu.CompilerParams(
            collective_id=0, has_side_effects=True, vmem_limit_bytes=60 * 1024 * 1024
        ),
    )
    return call(
        low_rank.T, q_base, k_base, v_base, edit_up, log_decay.T,
        norm_gain.reshape(heads, dh), lengths,
    )


def solution(mesh):
    rows = P(("ctx", "inner"), None)
    return jax.shard_map(
        shards,
        mesh=mesh,
        in_specs=(rows, rows, rows, rows, P(), rows, P("ctx"), P()),
        out_specs=rows,
        check_vma=False,
    )
```

time: 114 us -> 102 us (0.89)
  the two profiles are of different devices: /device:TPU:4 before, /device:TPU:704 now
where the time goes in v2:
time: 102 us; the launch traced here: 101 us
  Pallas kernels  98.2 us (96%)
  local copies, waits for them, and re-layouts  1.92 us (2%)
    pallas_call x1, Pallas kernels, shards(): call(low_rank.T, q_base, k_base, v_base, edit_up, log_decay.T, norm_gain....  98.2 us

profile of v2, /device:TPU:704, one launch (start us, length us, event | category | flops | bytes accessed | tf_op | source)
XLA Modules:
  0.0 100.8 jit_solution(18277936150350178555)
XLA Ops:
  0.7 98.2 %shard_map.82 = bf16[64,4608]{1,0:T(8,128)(2,1)} custom-call(bf16[32,64]{1,0:T(8,128)(2,1)} %bitcast.5, bf16[64,4608]{1,0:T(8,128)(2,1)} %q_hbm.1, bf16[64,4608]{1,0:T(8,128)(2,1)} %k_hbm.1, bf16[64,4608]{1,0:T(8,128)(2,1)} %v_hbm.1, bf16[32,13824]{1,0:T(8,128)(2,1)} %up_hbm.1, bf16[36,64]{1,0:T(8,128)(2,1)} %bitcast.4, f32[36,128]{1,0:T(8,128)} %bitcast.3, ...), custom_call_target="tpu_custom_call" | custom-call | tf_op jit(solution)/shard_map/pallas_call | solution.py:596
  98.8 1.9 %copy.11 = bf16[64,4608]{1,0:T(8,128)(2,1)} copy(bf16[64,4608]{1,0:T(8,128)(2,1)} %shard_map.82) | data formatting | bytes 1179648

commit v3 on v2

--- a/solution.py
+++ b/solution.py
@@ -264,9 +264,6 @@
             if s < rp:
                 reduce_step(plus_copy, ps_s, ps_r, s, owner_of(rp - s), k)
             reduce_step(minus_copy, ms_s, ms_r, s, owner_of(s - rm), k)
-            if s == 0 and k < hp - 1:
-                plus_copy(s, k).wait_send()
-                minus_copy(s, k).wait_send()
             chain(REDUCE_STEPS[k])
         if s == 0:
             keep_exp(2, before)
@@ -445,9 +442,6 @@
     for k in range(hp):
         ag_plus(0, z, k).start()
         ag_minus(0, z, k).start()
-        if k < hp - 1:
-            ag_plus(0, z, k).wait_send()
-            ag_minus(0, z, k).wait_send()
         chain(GATHER_STEPS[k])
     former_term(z)
     rest_p = -(-max(total_steps - progress["prior"], 0) // am)
@@ -495,14 +489,13 @@
 
     lax.fori_loop(1, zn, left_e, 0)
     for k in range(hp):
-        first = 0 if k == hp - 1 else 1
-        for s in range(first, rm):
+        for s in range(rm):
             minus_copy(s, k).wait_send()
-        for s in range(first, rp):
+        for s in range(rp):
             plus_copy(s, k).wait_send()
-        for s in range(first, am):
+        for s in range(am):
             ag_minus(s, owner_of(s), k).wait_send()
-        for s in range(first, ap):
+        for s in range(ap):
             ag_plus(s, owner_of(-s), k).wait_send()
 
     def left_r(i, carry):

time: 102 us -> 97.9 us (0.960)
  Pallas kernels: 98.2 us -> 95.1 us
    pallas_call x1, Pallas kernels: 98.2 us -> 95.1 us  [shards(): call(low_rank.T, q_base, k_base, v_base, edit_up, log_decay.T, norm_gain....]
where the time goes in v3:
time: 97.9 us; the launch traced here: 97.7 us
  Pallas kernels  95.1 us (97%)
  local copies, waits for them, and re-layouts  1.92 us (2%)
    pallas_call x1, Pallas kernels, shards(): call(low_rank.T, q_base, k_base, v_base, edit_up, log_decay.T, norm_gain....  95.1 us

profile of v3, /device:TPU:704, one launch (start us, length us, event | category | flops | bytes accessed | tf_op | source)
XLA Modules:
  0.0 97.7 jit_solution(9622836194595466310)
XLA Ops:
  0.7 95.1 %shard_map.82 = bf16[64,4608]{1,0:T(8,128)(2,1)} custom-call(bf16[32,64]{1,0:T(8,128)(2,1)} %bitcast.5, bf16[64,4608]{1,0:T(8,128)(2,1)} %q_hbm.1, bf16[64,4608]{1,0:T(8,128)(2,1)} %k_hbm.1, bf16[64,4608]{1,0:T(8,128)(2,1)} %v_hbm.1, bf16[32,13824]{1,0:T(8,128)(2,1)} %up_hbm.1, bf16[36,64]{1,0:T(8,128)(2,1)} %bitcast.4, f32[36,128]{1,0:T(8,128)} %bitcast.3, ...), custom_call_target="tpu_custom_call" | custom-call | tf_op jit(solution)/shard_map/pallas_call | solution.py:589
  95.7 1.9 %copy.11 = bf16[64,4608]{1,0:T(8,128)(2,1)} copy(bf16[64,4608]{1,0:T(8,128)(2,1)} %shard_map.82) | data formatting | bytes 1179648

commit v4 on v3

--- a/solution.py
+++ b/solution.py
@@ -18,7 +18,7 @@
 REDUCE_STEPS = (1, 1, 1)
 GATHER_STEPS = (1, 2, 1)
 UNITS = (8, 11)
-C_STEPS = (1, 1, 1, 1)
+C_STEPS = (0, 0, 0, 0)
 P_STEPS = 24
 
 

time: 97.9 us -> 99.2 us (1.013)
  Pallas kernels: 95.1 us -> 96.4 us
    pallas_call x1, Pallas kernels: 95.1 us -> 96.4 us  [shards(): call(low_rank.T, q_base, k_base, v_base, edit_up, log_decay.T, norm_gain....]
where the time goes in v4:
time: 99.2 us; the launch traced here: 99 us
  Pallas kernels  96.4 us (97%)
  local copies, waits for them, and re-layouts  1.92 us (2%)
    pallas_call x1, Pallas kernels, shards(): call(low_rank.T, q_base, k_base, v_base, edit_up, log_decay.T, norm_gain....  96.4 us

profile of v4, /device:TPU:704, one launch (start us, length us, event | category | flops | bytes accessed | tf_op | source)
XLA Modules:
  0.0 99.0 jit_solution(7794561446887430003)
XLA Ops:
  0.7 96.4 %shard_map.82 = bf16[64,4608]{1,0:T(8,128)(2,1)} custom-call(bf16[32,64]{1,0:T(8,128)(2,1)} %bitcast.5, bf16[64,4608]{1,0:T(8,128)(2,1)} %q_hbm.1, bf16[64,4608]{1,0:T(8,128)(2,1)} %k_hbm.1, bf16[64,4608]{1,0:T(8,128)(2,1)} %v_hbm.1, bf16[32,13824]{1,0:T(8,128)(2,1)} %up_hbm.1, bf16[36,64]{1,0:T(8,128)(2,1)} %bitcast.4, f32[36,128]{1,0:T(8,128)} %bitcast.3, ...), custom_call_target="tpu_custom_call" | custom-call | tf_op jit(solution)/shard_map/pallas_call | solution.py:589
  97.1 1.9 %copy.11 = bf16[64,4608]{1,0:T(8,128)(2,1)} copy(bf16[64,4608]{1,0:T(8,128)(2,1)} %shard_map.82) | data formatting | bytes 1179648

commit v5 on v3

--- a/solution.py
+++ b/solution.py
@@ -261,9 +261,9 @@
 
     for s in range(rm):
         for k in range(hp):
+            reduce_step(minus_copy, ms_s, ms_r, s, owner_of(s - rm), k)
             if s < rp:
                 reduce_step(plus_copy, ps_s, ps_r, s, owner_of(rp - s), k)
-            reduce_step(minus_copy, ms_s, ms_r, s, owner_of(s - rm), k)
             chain(REDUCE_STEPS[k])
         if s == 0:
             keep_exp(2, before)
@@ -440,8 +440,8 @@
             gac[:, at] = jnp.exp(dbc[:, at]) * factor(2, h) * inter
 
     for k in range(hp):
+        ag_minus(0, z, k).start()
         ag_plus(0, z, k).start()
-        ag_minus(0, z, k).start()
         chain(GATHER_STEPS[k])
     former_term(z)
     rest_p = -(-max(total_steps - progress["prior"], 0) // am)
@@ -450,13 +450,13 @@
         o_m = owner_of(s + 1)
         o_p = owner_of(-1 - s)
         for k in range(hp):
+            ag_minus(s, o_m, k).wait_recv()
+            if s + 1 < am:
+                ag_minus(s + 1, o_m, k).start()
             if s < ap:
                 ag_plus(s, o_p, k).wait_recv()
                 if s + 1 < ap:
                     ag_plus(s + 1, o_p, k).start()
-            ag_minus(s, o_m, k).wait_recv()
-            if s + 1 < am:
-                ag_minus(s + 1, o_m, k).start()
             chain(total_steps if s == final and k + 1 == hp else GATHER_STEPS[k])
         if s < ap:
             former_term(o_p)

time: 97.9 us -> 97.8 us (level)
  no operation moved by 1% of the time
where the time goes in v5:
time: 97.8 us; the launch traced here: 97.6 us
  Pallas kernels  95 us (97%)
  local copies, waits for them, and re-layouts  1.92 us (2%)
    pallas_call x1, Pallas kernels, shards(): call(low_rank.T, q_base, k_base, v_base, edit_up, log_decay.T, norm_gain....  95 us

profile of v5, /device:TPU:704, one launch (start us, length us, event | category | flops | bytes accessed | tf_op | source)
XLA Modules:
  0.0 97.6 jit_solution(16228456886567175294)
XLA Ops:
  0.7 95.0 %shard_map.82 = bf16[64,4608]{1,0:T(8,128)(2,1)} custom-call(bf16[32,64]{1,0:T(8,128)(2,1)} %bitcast.5, bf16[64,4608]{1,0:T(8,128)(2,1)} %q_hbm.1, bf16[64,4608]{1,0:T(8,128)(2,1)} %k_hbm.1, bf16[64,4608]{1,0:T(8,128)(2,1)} %v_hbm.1, bf16[32,13824]{1,0:T(8,128)(2,1)} %up_hbm.1, bf16[36,64]{1,0:T(8,128)(2,1)} %bitcast.4, f32[36,128]{1,0:T(8,128)} %bitcast.3, ...), custom_call_target="tpu_custom_call" | custom-call | tf_op jit(solution)/shard_map/pallas_call | solution.py:589
  95.6 1.9 %copy.11 = bf16[64,4608]{1,0:T(8,128)(2,1)} copy(bf16[64,4608]{1,0:T(8,128)(2,1)} %shard_map.82) | data formatting | bytes 1179648
